TPU v7x, 32 devices: a whole 2x2x4 slice. The times are simulated.
32 devices in a mesh: groups: 2 (over y), blk: 4 (over z), head: 2 (over x), pair: 2 (over core).
Axes of the slice: x: 2, y: 2, z: 4, core: 2. Of those that a mesh axis runs over, the one named last changes fastest.
Arguments:
- single: bfloat16 [256, 384], P(('groups', 'blk')), parts along dimension 0, may hold values from -6 to 6
- pair: bfloat16 [256, 4, 32, 128], P(('groups', 'blk'), None, 'pair'), parts along dimension 0, may hold values from -6 to 6
- frames: float32 [12, 256], P(None, ('groups', 'blk')), parts along dimension 1, as said below
- chain: int32 [256], P(('groups', 'blk')), parts along dimension 0, may hold values from 0 to 5, never falling along the last dimension, each value on 1 to 42 neighbouring positions
- mask: int32 [256], P(('groups', 'blk')), parts along dimension 0, may hold values 0 or 1
- w_query: bfloat16 [384, 192], P(None, 'head'), may hold values from -0.3125 to 0.3125
- w_key_value: bfloat16 [384, 384], P(None, 'head'), may hold values from -0.3125 to 0.3125
- w_query_points: bfloat16 [384, 144], P(None, 'head'), may hold values from -0.3125 to 0.3125
- w_kv_points: bfloat16 [384, 432], P(None, 'head'), may hold values from -0.3125 to 0.3125
- w_pair_bias: bfloat16 [128, 12], P(None, 'head'), may hold values from -0.5 to 0.5
- head_weights: float32 [12], P('head'), may hold values from -9 to 1
- chain_bias: float32 [12], P('head'), may hold values from -3 to 3
- w_out: bfloat16 [12, 176, 384], P('head'), may hold values from -0.125 to 0.125
- out_gain: float32 [384], replicated, may hold values from 0.5 to 1.5
- w_backbone: bfloat16 [384, 6], replicated, may hold values from -0.3125 to 0.3125
Outputs:
- single_out: bfloat16 [256, 384], P(('groups', 'blk')), parts along dimension 0
- frames_out: float32 [12, 256], P(None, 'groups'), parts along dimension 1
There are 2 independent parts, one for each index of `groups`. A program takes and returns all parts, laid end to end along the dimension named above; an argument that names none is the same for every part. Nothing has to cross between parts.
Inputs may be any that keep to these rules, and one draw needn't show every extreme that they name: `frames`: rows 0 to 8 of every column hold an orthonormal rotation matrix row by row; rows 9 to 11 the translation.
All inputs are finite; a program needn't handle non-finite values. No bound on the sum of `mask` on one device may be relied on, other than what follows from the above.
Results may differ from a plain program's by a relative error of at most 0.0048.
Values sent between devices are 32-bit elements; how exact they have to be, the bound alone decides.
A program may use at most 64 MiB of HBM per device.

v0:
```python
import math
import jax
import jax.numpy as jnp
from jax import lax
from jax.sharding import PartitionSpec as P

HIGH = lax.Precision.HIGHEST
LOGIT_WEIGHT = math.sqrt(1.0 / 3.0)
MASK_PENALTY = 100000.0


def shifted(array, axis, by):
    peers = lax.axis_size(axis)
    return lax.ppermute(array, axis, [(i, (i + by) % peers) for i in range(peers)])


def combined_all(value, axis, join):
    pieces = jax.tree.map(lambda part: lax.all_gather(part, axis), value)
    head = jax.tree.map(lambda part: part[0], pieces)
    tail = jax.tree.map(lambda part: part[1:], pieces)
    so_far, _ = lax.scan(lambda so_far, section: (join(so_far, section), None), head, tail)
    return so_far


def to_global(local, frames):
    rotation = frames[:9].reshape(3, 3, -1)
    moved = jnp.einsum("abn,ngb->nga", rotation, local, precision=HIGH)
    return moved + jnp.transpose(frames[9:12])[:, None, :]


def to_local(points, frames):
    rotation = frames[:9].reshape(3, 3, -1)
    moved = points - jnp.transpose(frames[9:12])[:, None, None, :]
    return jnp.einsum("abn,nhpa->nhpb", rotation, moved, precision=HIGH)


def compose(frames, motion):
    rotation = frames[:9].reshape(3, 3, -1)
    inverse = 1.0 / jnp.sqrt(1.0 + motion[:, 0] ** 2 + motion[:, 1] ** 2 + motion[:, 2] ** 2)
    quat_b = motion[:, 0] * inverse
    quat_c = motion[:, 1] * inverse
    quat_d = motion[:, 2] * inverse
    spin = jnp.stack(
        [
            inverse * inverse + quat_b * quat_b - quat_c * quat_c - quat_d * quat_d,
            2.0 * (quat_b * quat_c - inverse * quat_d),
            2.0 * (quat_b * quat_d + inverse * quat_c),
            2.0 * (quat_b * quat_c + inverse * quat_d),
            inverse * inverse - quat_b * quat_b + quat_c * quat_c - quat_d * quat_d,
            2.0 * (quat_c * quat_d - inverse * quat_b),
            2.0 * (quat_b * quat_d - inverse * quat_c),
            2.0 * (quat_c * quat_d + inverse * quat_b),
            inverse * inverse - quat_b * quat_b - quat_c * quat_c + quat_d * quat_d,
        ]
    ).reshape(3, 3, -1)
    new_rotation = jnp.einsum("abn,bcn->acn", rotation, spin, precision=HIGH)
    offset = jnp.einsum("abn,nb->an", rotation, motion[:, 3:6], precision=HIGH)
    return jnp.concatenate([new_rotation.reshape(9, -1), frames[9:12] + offset], axis=0)


def attention_logits(
    pair_rows,
    query_rows,
    query_points,
    query_chain,
    query_present,
    keys,
    key_points,
    key_chain,
    key_present,
    w_pair_bias,
    distance_scale,
    chain_bias,
):
    count_q = pair_rows.shape[0]
    count_k = pair_rows.shape[1]
    bias = jnp.dot(
        pair_rows.reshape(count_q * count_k, -1), w_pair_bias, preferred_element_type=jnp.float32
    ).reshape(count_q, count_k, -1)
    dots = jnp.einsum("ihc,jhc->ijh", query_rows, keys, precision=HIGH) / math.sqrt(keys.shape[-1])
    gaps = query_points[:, None] - key_points[None]
    distance = jnp.sum(gaps * gaps, axis=(3, 4))
    differ = (query_chain[:, None] != key_chain[None, :]).astype(jnp.float32)
    logits = LOGIT_WEIGHT * (
        dots + bias - distance_scale * distance + chain_bias * differ[..., None]
    )
    absent = 1.0 - query_present[:, None] * key_present[None, :]
    return logits - MASK_PENALTY * absent[..., None]


def rescale(values, factor):
    return values * factor.reshape(factor.shape + (1,) * (values.ndim - factor.ndim))


def fold_pair(first, second):
    best = jnp.maximum(first[0], second[0])
    first_scale = jnp.exp(first[0] - best)
    second_scale = jnp.exp(second[0] - best)
    merged = [
        rescale(left_part, first_scale) + rescale(right_part, second_scale)
        for left_part, right_part in zip(first[1:], second[1:])
    ]
    return (best,) + tuple(merged)


def body(
    single,
    pair,
    frames,
    chain,
    mask,
    w_query,
    w_key_value,
    w_query_points,
    w_kv_points,
    w_pair_bias,
    head_weights,
    chain_bias,
    w_out,
    out_gain,
    w_backbone,
):
    rows = single.shape[0]
    half = pair.shape[2]
    width = pair.shape[3]
    heads_here = w_pair_bias.shape[1]
    head_size = w_query.shape[1] // heads_here
    query_count = w_query_points.shape[1] // (3 * heads_here)
    value_count = w_kv_points.shape[1] // (3 * heads_here) - query_count
    pair_keys = pair.reshape(rows, pair.shape[1] * half, width)
    query = jnp.dot(single, w_query, preferred_element_type=jnp.float32).reshape(
        rows, heads_here, head_size
    )
    query_local = jnp.dot(single, w_query_points, preferred_element_type=jnp.float32)
    query_points = to_global(query_local.reshape(rows, heads_here * query_count, 3), frames)
    query_points = query_points.reshape(rows, heads_here, query_count, 3)
    query_chain = chain.astype(jnp.float32)
    query_present = mask.astype(jnp.float32)
    distance_scale = jax.nn.softplus(head_weights) * math.sqrt(2.0 / (9.0 * query_count)) / 2.0
    position = lax.axis_index("pair")
    key_single = lax.dynamic_slice_in_dim(single, position * half, half, 0)
    key_frames = lax.dynamic_slice_in_dim(frames, position * half, half, 1)
    key_chain = lax.dynamic_slice_in_dim(query_chain, position * half, half, 0)
    key_present = lax.dynamic_slice_in_dim(query_present, position * half, half, 0)
    key_value = jnp.dot(key_single, w_key_value, preferred_element_type=jnp.float32)
    key_local = jnp.dot(key_single, w_kv_points, preferred_element_type=jnp.float32)
    key_global = to_global(
        key_local.reshape(half, heads_here * (query_count + value_count), 3), key_frames
    )
    payload = jnp.concatenate([key_value, key_global.reshape(half, -1)], axis=1)
    key_meta = jnp.stack([key_chain, key_present], axis=1)
    split_at = heads_here * 2 * head_size

    def absorb(carry, moving, moving_meta, start):
        top, total, sum_values, sum_points, sum_pair = carry
        count = moving.shape[0]
        pieces = moving[:, :split_at].reshape(count, heads_here, 2, head_size)
        points = moving[:, split_at:].reshape(count, heads_here, query_count + value_count, 3)
        pair_rows = lax.dynamic_slice_in_dim(pair_keys, start, count, 1)
        logits = attention_logits(
            pair_rows,
            query,
            query_points,
            query_chain,
            query_present,
            pieces[:, :, 0],
            points[:, :, :query_count],
            moving_meta[:, 0],
            moving_meta[:, 1],
            w_pair_bias,
            distance_scale,
            chain_bias,
        )
        new_top = jnp.maximum(top, jnp.max(logits, axis=1))
        scale = jnp.exp(top - new_top)
        weights = jnp.exp(logits - new_top[:, None, :])
        total = total * scale + jnp.sum(weights, axis=1)
        sum_values = sum_values * scale[..., None] + jnp.einsum(
            "ijh,jhc->ihc", weights, pieces[:, :, 1], precision=HIGH
        )
        sum_points = sum_points * scale[..., None, None] + jnp.einsum(
            "ijh,jhpd->ihpd", weights, points[:, :, query_count:], precision=HIGH
        )
        sum_pair = sum_pair * scale[..., None] + jnp.einsum(
            "ijh,ijc->ihc",
            weights.astype(jnp.bfloat16),
            pair_rows,
            preferred_element_type=jnp.float32,
        )
        return (new_top, total, sum_values, sum_points, sum_pair)

    initial = (
        jnp.full((rows, heads_here), -1e30, jnp.float32),
        jnp.zeros((rows, heads_here), jnp.float32),
        jnp.zeros((rows, heads_here, head_size), jnp.float32),
        jnp.zeros((rows, heads_here, value_count, 3), jnp.float32),
        jnp.zeros((rows, heads_here, width), jnp.float32),
    )
    block = lax.axis_index("blk")
    blocks = lax.axis_size("blk")
    carry = absorb(initial, payload, key_meta, block * half)

    def advance(step, state):
        carry, moving, moving_meta = state
        moving, moving_meta = shifted((moving, moving_meta), "blk", 1)
        source = (block - step) % blocks
        return (absorb(carry, moving, moving_meta, source * half), moving, moving_meta)

    carry = lax.fori_loop(1, blocks, advance, (carry, payload, key_meta))[0]
    best, total, sum_values, sum_points, sum_pair = combined_all(carry, "pair", fold_pair)
    attended = sum_values / total[..., None]
    pointed = to_local(sum_points / total[..., None, None], frames)
    point_norms = jnp.sqrt(jnp.sum(pointed * pointed, axis=3) + 1.0)
    paired = sum_pair / total[..., None]
    joined = jnp.concatenate(
        [attended, pointed.reshape(rows, heads_here, value_count * 3), point_norms, paired], axis=2
    ).astype(jnp.bfloat16)
    partial_update = jnp.dot(
        joined.reshape(rows, -1),
        w_out.reshape(-1, w_out.shape[2]),
        preferred_element_type=jnp.float32,
    )
    update = lax.psum(partial_update, "head")
    mixed = single.astype(jnp.float32) + update
    centre = jnp.mean(mixed, axis=1, keepdims=True)
    spread = jnp.mean(jnp.square(mixed - centre), axis=1, keepdims=True)
    single_out = ((mixed - centre) * lax.rsqrt(spread + 1e-05) * out_gain).astype(jnp.bfloat16)
    motion = jnp.dot(single_out, w_backbone, preferred_element_type=jnp.float32)
    frames_new = compose(frames, motion)
    frames_out = lax.all_gather(frames_new, "blk", axis=1, tiled=True)
    return (single_out, frames_out)


def solution(mesh):
    placed = (
        P(("groups", "blk"), None),
        P(("groups", "blk"), None, "pair", None),
        P(None, ("groups", "blk")),
        P(("groups", "blk")),
        P(("groups", "blk")),
        P(None, "head"),
        P(None, "head"),
        P(None, "head"),
        P(None, "head"),
        P(None, "head"),
        P("head"),
        P("head"),
        P("head", None, None),
        P(),
        P(),
    )
    return jax.shard_map(
        body,
        mesh=mesh,
        in_specs=placed,
        out_specs=(P(("groups", "blk"), None), P(None, "groups")),
        check_vma=False,
    )
```

profile of v0, /device:TPU:0, one launch (start us, length us, event | category | flops | bytes accessed | tf_op | source)
XLA Modules:
  0.0 85.5 jit_solution(7720689807309747148)
XLA Ops:
  0.7 0.7 copy-done.13
  1.7 0.3 copy-done.8
  2.6 0.6 copy-done.3
  3.1 1.1 %fusion.59 = f32[16,192]{1,0:T(8,128)S(1)} fusion(bf16[384,192]{0,1:T(8,128)(2,1)} %param.23, bf16[32,384]{1,0:T(8,128)(2,1)S(1)} %copy-done.3, s32[]{:T(128)S(6)} %select_n.43), kind=kOutput, calls=%fused_computation.96 | convolution fusion | flops 2359296 | bytes 172036 | tf_op jit(solution)/shard_map/dot_general | solution.py:145
  4.6 0.8 copy-done.7
  5.7 0.3 convolution_add_fusion.2
  6.6 0.7 copy-done.4
  7.7 0.3 convolution_add_fusion.3
  8.4 0.3 copy-done.2
  8.7 0.3 copy-done.6
  9.0 0.4 fusion.35
  9.6 0.2 copy.240
  9.8 0.2 multiply_reduce_fusion.1
  10.1 0.4 copy-done.10
  10.5 0.2 fusion.84
  11.6 0.4 fusion.20
  12.0 35.5 %while.7 = (s32[]{:T(128)}, f32[32,6]{0,1:T(8,128)S(1)}, f32[32,6]{0,1:T(8,128)S(1)}, f32[32,6,16]{0,2,1:T(8,128)S(1)}, f32[32,6,8,3]{0,2,3,1:T(8,128)S(1)}, /*i...) while((s32[]{:T(128)}, f32[32,6]{0,1:T(8,128)S(1)}, ...), condition=%wide.region_7.8_spmd, body=%wide.region_3.7_spmd.sunk | while | flops 3855250 | bytes 1648512 | solution.py:209
  12.0 3.1 %collective-permute-start = (f32[16,2]{0,1:T(2,128)S(1)}, f32[16,2]{0,1:T(2,128)S(1)}, u32[]{:S(2)}, u32[]{:S(2)}) collective-permute-start(f32[16,2]{0,1:T(2,128)S(1)} %get-tuple-element.757), channel_id=1, source_target_pairs={{0,4},{4,8},{8,12},{12,0},{1,5},{5,9},{9,13},{13,1},{2,6},{6,10},{... | collective-permute-start | bytes 392 | tf_op jit(solution)/shard_map/while/body/eval_jaxpr/ppermute | solution.py:14
  15.1 1.6 %collective-permute-start.1 = (f32[16,408]{0,1:T(8,128)S(1)}, f32[16,408]{0,1:T(8,128)S(1)}, u32[]{:S(2)}, u32[]{:S(2)}) collective-permute-start(f32[16,408]{0,1:T(8,128)S(1)} %get-tuple-element.756), channel_id=1, source_target_pairs={{0,4},{4,8},{8,12},{12,0},{1,5},{5,9},{9,13},{13,1},{2,6},{6,10},{... | collective-permute-start | bytes 78344 | tf_op jit(solution)/shard_map/while/body/eval_jaxpr/ppermute | solution.py:14
  16.7 0.4 fusion.127
  17.2 1.5 %collective-permute-done = f32[16,2]{0,1:T(2,128)S(1)} collective-permute-done((f32[16,2]{0,1:T(2,128)S(1)}, f32[16,2]{0,1:T(2,128)S(1)}, u32[]{:S(2)}, u32[]{:S(2)}) %collective-permute-start) | collective-permute-done | bytes 160 | tf_op jit(solution)/shard_map/while/body/eval_jaxpr/ppermute | solution.py:14
  18.9 4.7 %collective-permute-done.1 = f32[16,408]{0,1:T(8,128)S(1)} collective-permute-done((f32[16,408]{0,1:T(8,128)S(1)}, f32[16,408]{0,1:T(8,128)S(1)}, u32[]{:S(2)}, u32[]{:S(2)}) %collective-permute-start.1) | collective-permute-done | bytes 26144 | tf_op jit(solution)/shard_map/while/body/eval_jaxpr/ppermute | solution.py:14
  23.7 0.6 copy-done.1
  24.3 0.2 multiply_reduce_fusion.6
  24.5 0.3 fusion.128
  25.3 0.6 slice-done
  25.9 0.3 fusion.131
  26.2 0.2 convolution_add_fusion.5
  26.5 1.4 %collective-permute-start.1 = (f32[16,408]{0,1:T(8,128)S(1)}, f32[16,408]{0,1:T(8,128)S(1)}, u32[]{:S(2)}, u32[]{:S(2)}) collective-permute-start(f32[16,408]{0,1:T(8,128)S(1)} %get-tuple-element.756), channel_id=1, source_target_pairs={{0,4},{4,8},{8,12},{12,0},{1,5},{5,9},{9,13},{13,1},{2,6},{6,10},{... | collective-permute-start | bytes 78344 | tf_op jit(solution)/shard_map/while/body/eval_jaxpr/ppermute | solution.py:14
  27.8 0.4 fusion.127
  28.3 3.5 %collective-permute-done = f32[16,2]{0,1:T(2,128)S(1)} collective-permute-done((f32[16,2]{0,1:T(2,128)S(1)}, f32[16,2]{0,1:T(2,128)S(1)}, u32[]{:S(2)}, u32[]{:S(2)}) %collective-permute-start) | collective-permute-done | bytes 160 | tf_op jit(solution)/shard_map/while/body/eval_jaxpr/ppermute | solution.py:14
  32.0 2.1 %collective-permute-done.1 = f32[16,408]{0,1:T(8,128)S(1)} collective-permute-done((f32[16,408]{0,1:T(8,128)S(1)}, f32[16,408]{0,1:T(8,128)S(1)}, u32[]{:S(2)}, u32[]{:S(2)}) %collective-permute-start.1) | collective-permute-done | bytes 26144 | tf_op jit(solution)/shard_map/while/body/eval_jaxpr/ppermute | solution.py:14
  34.2 0.6 copy-done.1
  34.9 0.2 multiply_reduce_fusion.6
  35.1 0.3 fusion.128
  35.9 0.6 slice-done
  36.4 0.3 fusion.131
  36.7 0.2 convolution_add_fusion.5
  37.1 0.6 collective-permute-start.1
  37.7 0.4 fusion.127
  38.2 4.3 %collective-permute-done = f32[16,2]{0,1:T(2,128)S(1)} collective-permute-done((f32[16,2]{0,1:T(2,128)S(1)}, f32[16,2]{0,1:T(2,128)S(1)}, u32[]{:S(2)}, u32[]{:S(2)}) %collective-permute-start) | collective-permute-done | bytes 160 | tf_op jit(solution)/shard_map/while/body/eval_jaxpr/ppermute | solution.py:14
  42.6 2.1 %collective-permute-done.1 = f32[16,408]{0,1:T(8,128)S(1)} collective-permute-done((f32[16,408]{0,1:T(8,128)S(1)}, f32[16,408]{0,1:T(8,128)S(1)}, u32[]{:S(2)}, u32[]{:S(2)}) %collective-permute-start.1) | collective-permute-done | bytes 26144 | tf_op jit(solution)/shard_map/while/body/eval_jaxpr/ppermute | solution.py:14
  44.8 0.6 copy-done.1
  45.4 0.2 multiply_reduce_fusion.6
  45.7 0.3 fusion.128
  46.4 0.6 slice-done
  47.0 0.3 fusion.131
  47.3 0.2 convolution_add_fusion.5
  47.6 1.8 %all-gather.5 = f32[2,32,6]{1,2,0:T(8,128)S(1)} all-gather(f32[1,32,6]{1,2,0:T(8,128)S(1)} %bitcast.281), channel_id=3, replica_groups=mesh['groups'=2,'blk'=4,'head'=2,'pair'=2] {'pair'}, dimensions={0}, use_global_device_ids=true | all-gather | bytes 2304 | tf_op jit(solution)/shard_map/all_gather | solution.py:18
  49.4 1.8 %all-gather.6 = f32[2,32,6]{1,2,0:T(8,128)S(1)} all-gather(f32[1,32,6]{1,2,0:T(8,128)S(1)} %bitcast.282), channel_id=4, replica_groups=mesh['groups'=2,'blk'=4,'head'=2,'pair'=2] {'pair'}, dimensions={0}, use_global_device_ids=true | all-gather | bytes 2304 | tf_op jit(solution)/shard_map/all_gather | solution.py:18
  51.5 1.9 %all-gather.4 = f32[64,6,128]{2,0,1:T(8,128)S(1)} all-gather(f32[32,6,128]{2,0,1:T(8,128)S(1)} %copy.259), channel_id=6, replica_groups=mesh['groups'=2,'blk'=4,'head'=2,'pair'=2] {'pair'}, dimensions={0}, use_global_device_ids=true | all-gather | bytes 294912 | tf_op jit(solution)/shard_map/all_gather | solution.py:18
  53.7 1.9 %all-gather = f32[64,6,16]{2,0,1:T(8,128)S(1)} all-gather(f32[32,6,16]{2,0,1:T(8,128)S(1)} %copy.249), channel_id=2, replica_groups=mesh['groups'=2,'blk'=4,'head'=2,'pair'=2] {'pair'}, dimensions={0}, use_global_device_ids=true | all-gather | bytes 36864 | tf_op jit(solution)/shard_map/all_gather | solution.py:18
  55.8 0.2 copy.250
  56.0 2.4 %all-gather.3 = f32[64,6,8,3]{2,1,3,0:T(8,128)S(1)} all-gather(f32[32,6,8,3]{2,1,3,0:T(8,128)S(1)} %copy.250), channel_id=5, replica_groups=mesh['groups'=2,'blk'=4,'head'=2,'pair'=2] {'pair'}, dimensions={0}, use_global_device_ids=true | all-gather | bytes 55296 | tf_op jit(solution)/shard_map/all_gather | solution.py:18
  58.4 0.3 fusion.30
  58.6 1.1 %fusion.82 = (bf16[32,6,8,3]{2,3,1,0:T(4,128)(2,1)S(1)}, f32[32,6,8]{2,1,0:T(8,128)S(1)}) fusion(f32[3,3,32,1]{0,1,3,2:T(4,128)S(1)} %copy.271, f32[32,6,8,3]{2,1,3,0:T(8,128)S(1)} %fusion.30), kind=kOutput, calls=%fused_computation.152 | convolution fusion | flops 178176 | bytes 34944 | tf_op jit(solution)/shard_map/abn,nhpa->nhpb/dot_general | solution.py:34
  59.7 0.2 copy.257
  60.3 0.4 convolution_bitcast_fusion.4
  60.7 8.6 %psum.7 = f32[32,384]{1,0:T(8,128)S(1)} all-reduce(f32[32,384]{1,0:T(8,128)S(1)} %convolution_bitcast_fusion.4), channel_id=1, replica_groups=mesh['groups'=2,'blk'=4,'head'=2,'pair'=2] {'head'}, use_global_device_ids=true, to_apply=%region_9.10 | all-reduce | flops 12288 | bytes 98304 | tf_op jit(solution)/shard_map/psum | solution.py:223
  69.7 0.6 copy-done.11
  70.5 0.4 copy-done.5
  71.1 0.3 convolution_bitcast_fusion.3
  71.6 13.1 %all-gather.7 = f32[4,32,12]{1,2,0:T(8,128)S(1)} all-gather(f32[1,32,12]{1,2,0:T(8,128)S(1)} %maximum_bitcast_fusion), channel_id=1, replica_groups=mesh['groups'=2,'blk'=4,'head'=2,'pair'=2] {'blk'}, dimensions={0}, use_global_device_ids=true | all-gather | bytes 7680 | tf_op jit(solution)/shard_map/all_gather | solution.py:230
  84.8 0.7 reshape.714
  (160 shorter events, 8.1 us)
Async XLA Ops:
  0.6 59.6 %copy-start = (bf16[6,176,384]{2,1,0:T(8,128)(2,1)S(1)}, bf16[6,176,384]{2,1,0:T(8,128)(2,1)}, u32[]{:S(2)}) copy-start(bf16[6,176,384]{2,1,0:T(8,128)(2,1)} %param.29) | copy-start | bytes 2433028
  0.7 0.7 copy-start.13
  0.7 0.7 copy-start.14
  0.7 0.7 copy-start.15
  1.4 0.7 copy-start.8
  2.4 0.7 copy-start.3
  3.1 1.2 %copy-start.9 = (bf16[384,72]{0,1:T(8,128)(2,1)S(1)}, bf16[384,72]{0,1:T(8,128)(2,1)}, u32[]{:S(2)}) copy-start(bf16[384,72]{0,1:T(8,128)(2,1)} %param.24) | copy-start | bytes 165892
  4.5 0.9 %copy-start.7 = (bf16[384,96]{0,1:T(8,128)(2,1)S(1)}, bf16[384,96]{0,1:T(8,128)(2,1)}, u32[]{:S(2)}) copy-start(bf16[384,96]{0,1:T(8,128)(2,1)} %param.22) | copy-start | bytes 221188
  6.5 0.9 %copy-start.4 = (bf16[384,216]{0,1:T(8,128)(2,1)S(1)}, bf16[384,216]{0,1:T(8,128)(2,1)}, u32[]{:S(2)}) copy-start(bf16[384,216]{0,1:T(8,128)(2,1)} %param.25) | copy-start | bytes 497668
  7.6 1.0 %copy-start.2 = (bf16[32,4,16,128]{3,2,1,0:T(8,128)(2,1)S(1)}, bf16[32,4,16,128]{3,2,1,0:T(8,128)(2,1)}, u32[]{:S(2)}) copy-start(bf16[32,4,16,128]{3,2,1,0:T(8,128)(2,1)} %param.18) | copy-start | bytes 1572868
  8.3 0.7 copy-start.6
  9.8 0.7 copy-start.10
  12.0 6.7 %collective-permute-start = (f32[16,2]{0,1:T(2,128)S(1)}, f32[16,2]{0,1:T(2,128)S(1)}, u32[]{:S(2)}, u32[]{:S(2)}) collective-permute-start(f32[16,2]{0,1:T(2,128)S(1)} %get-tuple-element.757), channel_id=1, source_target_pairs={{0,4},{4,8},{8,12},{12,0},{1,5},{5,9},{9,13},{13,1},{2,6},{6,10},{... | collective-permute-start | bytes 392 | tf_op jit(solution)/shard_map/while/body/eval_jaxpr/ppermute | solution.py:14
  15.1 8.4 %collective-permute-start.1 = (f32[16,408]{0,1:T(8,128)S(1)}, f32[16,408]{0,1:T(8,128)S(1)}, u32[]{:S(2)}, u32[]{:S(2)}) collective-permute-start(f32[16,408]{0,1:T(8,128)S(1)} %get-tuple-element.756), channel_id=1, source_target_pairs={{0,4},{4,8},{8,12},{12,0},{1,5},{5,9},{9,13},{13,1},{2,6},{6,10},{... | collective-permute-start | bytes 78344 | tf_op jit(solution)/shard_map/while/body/eval_jaxpr/ppermute | solution.py:14
  23.6 0.7 copy-start.1
  25.0 0.9 %slice-start = ((f32[16,6,12,3]{0,3,2,1:T(4,128)}), f32[16,6,8,3]{0,3,2,1:T(4,128)S(1)}, s32[]{:S(2)}) async-start(f32[16,6,12,3]{0,3,2,1:T(4,128)} %copy-done.1), calls=%async_computation | async-start | bytes 196608 | tf_op jit(solution)/shard_map/while/body/eval_jaxpr/slice | solution.py:182
  26.4 5.4 %collective-permute-start = (f32[16,2]{0,1:T(2,128)S(1)}, f32[16,2]{0,1:T(2,128)S(1)}, u32[]{:S(2)}, u32[]{:S(2)}) collective-permute-start(f32[16,2]{0,1:T(2,128)S(1)} %get-tuple-element.757), channel_id=1, source_target_pairs={{0,4},{4,8},{8,12},{12,0},{1,5},{5,9},{9,13},{13,1},{2,6},{6,10},{... | collective-permute-start | bytes 392 | tf_op jit(solution)/shard_map/while/body/eval_jaxpr/ppermute | solution.py:14
  26.5 7.7 %collective-permute-start.1 = (f32[16,408]{0,1:T(8,128)S(1)}, f32[16,408]{0,1:T(8,128)S(1)}, u32[]{:S(2)}, u32[]{:S(2)}) collective-permute-start(f32[16,408]{0,1:T(8,128)S(1)} %get-tuple-element.756), channel_id=1, source_target_pairs={{0,4},{4,8},{8,12},{12,0},{1,5},{5,9},{9,13},{13,1},{2,6},{6,10},{... | collective-permute-start | bytes 78344 | tf_op jit(solution)/shard_map/while/body/eval_jaxpr/ppermute | solution.py:14
  34.2 0.7 copy-start.1
  35.6 0.9 %slice-start = ((f32[16,6,12,3]{0,3,2,1:T(4,128)}), f32[16,6,8,3]{0,3,2,1:T(4,128)S(1)}, s32[]{:S(2)}) async-start(f32[16,6,12,3]{0,3,2,1:T(4,128)} %copy-done.1), calls=%async_computation | async-start | bytes 196608 | tf_op jit(solution)/shard_map/while/body/eval_jaxpr/slice | solution.py:182
  37.0 5.4 %collective-permute-start = (f32[16,2]{0,1:T(2,128)S(1)}, f32[16,2]{0,1:T(2,128)S(1)}, u32[]{:S(2)}, u32[]{:S(2)}) collective-permute-start(f32[16,2]{0,1:T(2,128)S(1)} %get-tuple-element.757), channel_id=1, source_target_pairs={{0,4},{4,8},{8,12},{12,0},{1,5},{5,9},{9,13},{13,1},{2,6},{6,10},{... | collective-permute-start | bytes 392 | tf_op jit(solution)/shard_map/while/body/eval_jaxpr/ppermute | solution.py:14
  37.1 7.7 %collective-permute-start.1 = (f32[16,408]{0,1:T(8,128)S(1)}, f32[16,408]{0,1:T(8,128)S(1)}, u32[]{:S(2)}, u32[]{:S(2)}) collective-permute-start(f32[16,408]{0,1:T(8,128)S(1)} %get-tuple-element.756), channel_id=1, source_target_pairs={{0,4},{4,8},{8,12},{12,0},{1,5},{5,9},{9,13},{13,1},{2,6},{6,10},{... | collective-permute-start | bytes 78344 | tf_op jit(solution)/shard_map/while/body/eval_jaxpr/ppermute | solution.py:14
  44.8 0.7 copy-start.1
  46.1 0.9 %slice-start = ((f32[16,6,12,3]{0,3,2,1:T(4,128)}), f32[16,6,8,3]{0,3,2,1:T(4,128)S(1)}, s32[]{:S(2)}) async-start(f32[16,6,12,3]{0,3,2,1:T(4,128)} %copy-done.1), calls=%async_computation | async-start | bytes 196608 | tf_op jit(solution)/shard_map/while/body/eval_jaxpr/slice | solution.py:182
  60.3 9.3 %copy-start.12 = (f32[384]{0:T(512)S(1)}, f32[384]{0:T(512)}, u32[]{:S(2)}) copy-start(f32[384]{0:T(512)} %param.30) | copy-start | bytes 4612
  69.6 0.7 copy-start.11
  70.3 0.6 copy-start.5
where the time goes:
time: 86 us; the launch traced here: 85.5 us
  blocking collectives  31.6 us (37%)
  waiting for transfers between devices  18.2 us (21%)
  local copies, waits for them, and re-layouts  15 us (17%)
  matrix products  9.58 us (11%)
  starting transfers between devices  6.74 us (8%)
  other arithmetic  2.83 us (3%)
  between operations  1.1 us (1%)
    ppermute x6, waiting for transfers between devices, shifted(): lax.ppermute(array, axis, [(i, (i + by) % peers) for i in range(peers)])  18.2 us
    all_gather x1, blocking collectives, body(): frames_out = lax.all_gather(frames_new, 'blk', axis=1, tiled=True)  13.1 us
    all_gather x5, blocking collectives, combined_all(): pieces = jax.tree.map(lambda part: lax.all_gather(part, axis), value)  9.88 us
    psum x1, blocking collectives, body(): update = lax.psum(partial_update, 'head')  8.59 us
    ppermute x6, starting transfers between devices, shifted(): lax.ppermute(array, axis, [(i, (i + by) % peers) for i in range(peers)])  6.74 us
    unnamed x32, local copies, waits for them, and re-layouts  6.07 us
    while x15, local copies, waits for them, and re-layouts  1.94 us
    slice x7, local copies, waits for them, and re-layouts, absorb(): points[:, :, query_count:]  1.86 us
  transfers between devices with their start and end apart: 6, of which 6 were waited for; matrix products, arithmetic and copies ran while one was open for 2% of the time, Pallas kernels for 0%

commit v1 on v0

--- a/solution.py
+++ b/solution.py
@@ -227,7 +227,14 @@
     single_out = ((mixed - centre) * lax.rsqrt(spread + 1e-05) * out_gain).astype(jnp.bfloat16)
     motion = jnp.dot(single_out, w_backbone, preferred_element_type=jnp.float32)
     frames_new = compose(frames, motion)
-    frames_out = lax.all_gather(frames_new, "blk", axis=1, tiled=True)
+    size = lax.axis_size("blk")
+    right = [(i_2, (i_2 + 1) % size) for i_2 in range(size)]
+    parts = [frames_new]
+    for far in range(1, size):
+        parts = [lax.ppermute(parts[0], "blk", right), *parts]
+    whole = jnp.concatenate(parts, axis=1)
+    turn = (lax.axis_index("blk") + 1) * parts[-1].shape[1]
+    frames_out = jnp.roll(whole, turn, axis=1)
     return (single_out, frames_out)
 
 

time: 86 us -> 90.1 us (1.048)
  waiting for transfers between devices: 18.2 us -> 34.6 us
  blocking collectives: 31.6 us -> 18.5 us
    ppermute x0 -> x3, waiting for transfers between devices: none -> 16.3 us  [body(): parts = [lax.ppermute(parts[0], 'blk', right), *parts]]
    all_gather x1 -> x0, blocking collectives: 13.1 us -> none  [body(): frames_out = lax.all_gather(frames_new, 'blk', axis=1, tiled=True)]
    dot_general x1, matrix products: 1.06 us -> 0.16 us  [body(): jnp.dot(key_single, w_key_value, preferred_element_type=jnp.float32)]
    unnamed x32 -> x31, local copies, waits for them, and re-layouts: 6.07 us -> 6.22 us
  transfers between devices with their start and end apart: 6 -> 9, of which waited for: 6 -> 9; matrix products, arithmetic and copies ran while one was open for 2% -> 2% of each run, Pallas kernels for 0% -> 0%
where the time goes in v1:
time: 90.1 us; the launch traced here: 89.5 us
  waiting for transfers between devices  34.6 us (38%)
  blocking collectives  18.5 us (21%)
  local copies, waits for them, and re-layouts  15.9 us (18%)
  matrix products  9.48 us (11%)
  starting transfers between devices  6.79 us (8%)
  other arithmetic  2.83 us (3%)
  between operations  1.11 us (1%)
    ppermute x6, waiting for transfers between devices, shifted(): lax.ppermute(array, axis, [(i, (i + by) % peers) for i in range(peers)])  18.2 us
    ppermute x3, waiting for transfers between devices, body(): parts = [lax.ppermute(parts[0], 'blk', right), *parts]  16.3 us
    all_gather x5, blocking collectives, combined_all(): pieces = jax.tree.map(lambda part: lax.all_gather(part, axis), value)  9.88 us
    psum x1, blocking collectives, body(): update = lax.psum(partial_update, 'head')  8.6 us
    ppermute x6, starting transfers between devices, shifted(): lax.ppermute(array, axis, [(i, (i + by) % peers) for i in range(peers)])  6.72 us
    unnamed x31, local copies, waits for them, and re-layouts  6.22 us
    while x15, local copies, waits for them, and re-layouts  1.94 us
    slice x7, local copies, waits for them, and re-layouts, absorb(): points[:, :, query_count:]  1.86 us
  transfers between devices with their start and end apart: 9, of which 9 were waited for; matrix products, arithmetic and copies ran while one was open for 2% of the time, Pallas kernels for 0%

profile of v1, /device:TPU:0, one launch (start us, length us, event | category | flops | bytes accessed | tf_op | source)
XLA Modules:
  0.0 89.5 jit_solution(17439933111564739573)
XLA Ops:
  0.7 0.7 copy-done.13
  1.5 0.6 copy-done.14
  2.4 0.6 copy-done.3
  3.0 1.0 %fusion.86 = f32[32,72]{0,1:T(8,128)S(1)} fusion(bf16[32,384]{1,0:T(8,128)(2,1)S(1)} %copy-done.3, bf16[384,72]{0,1:T(8,128)(2,1)} %param.24), kind=kOutput, calls=%fused_computation.157 | convolution fusion | flops 1769472 | bytes 89088 | tf_op jit(solution)/shard_map/dot_general | solution.py:134
  4.2 0.3 convolution_add_fusion.2
  5.0 0.4 copy-done.4
  5.8 0.3 convolution_add_fusion.3
  6.3 0.6 copy-done.15
  7.2 0.7 copy-done.8
  8.8 0.4 copy-done.2
  9.2 0.3 copy-done.7
  9.5 0.4 fusion.35
  10.2 0.2 copy.197
  10.5 0.2 multiply_reduce_fusion.1
  10.7 0.6 copy-done.10
  12.2 0.4 fusion.20
  12.8 35.5 %while.7 = (s32[]{:T(128)}, f32[32,6]{0,1:T(8,128)S(1)}, f32[32,6]{0,1:T(8,128)S(1)}, f32[32,6,16]{0,2,1:T(8,128)S(1)}, f32[32,6,8,3]{0,2,3,1:T(8,128)S(1)}, /*i...) while((s32[]{:T(128)}, f32[32,6]{0,1:T(8,128)S(1)}, ...), condition=%wide.region_7.8_spmd, body=%wide.region_3.7_spmd.sunk | while | flops 3855250 | bytes 1648512 | solution.py:209
  12.8 3.1 %collective-permute-start = (f32[16,2]{0,1:T(2,128)S(1)}, f32[16,2]{0,1:T(2,128)S(1)}, u32[]{:S(2)}, u32[]{:S(2)}) collective-permute-start(f32[16,2]{0,1:T(2,128)S(1)} %get-tuple-element.740), channel_id=1, source_target_pairs={{0,4},{4,8},{8,12},{12,0},{1,5},{5,9},{9,13},{13,1},{2,6},{6,10},{... | collective-permute-start | bytes 392 | tf_op jit(solution)/shard_map/while/body/eval_jaxpr/ppermute | solution.py:14
  15.9 1.6 %collective-permute-start.1 = (f32[16,408]{0,1:T(8,128)S(1)}, f32[16,408]{0,1:T(8,128)S(1)}, u32[]{:S(2)}, u32[]{:S(2)}) collective-permute-start(f32[16,408]{0,1:T(8,128)S(1)} %get-tuple-element.739), channel_id=1, source_target_pairs={{0,4},{4,8},{8,12},{12,0},{1,5},{5,9},{9,13},{13,1},{2,6},{6,10},{... | collective-permute-start | bytes 78344 | tf_op jit(solution)/shard_map/while/body/eval_jaxpr/ppermute | solution.py:14
  17.5 0.4 fusion.127
  18.0 1.5 %collective-permute-done = f32[16,2]{0,1:T(2,128)S(1)} collective-permute-done((f32[16,2]{0,1:T(2,128)S(1)}, f32[16,2]{0,1:T(2,128)S(1)}, u32[]{:S(2)}, u32[]{:S(2)}) %collective-permute-start) | collective-permute-done | bytes 160 | tf_op jit(solution)/shard_map/while/body/eval_jaxpr/ppermute | solution.py:14
  19.6 4.7 %collective-permute-done.1 = f32[16,408]{0,1:T(8,128)S(1)} collective-permute-done((f32[16,408]{0,1:T(8,128)S(1)}, f32[16,408]{0,1:T(8,128)S(1)}, u32[]{:S(2)}, u32[]{:S(2)}) %collective-permute-start.1) | collective-permute-done | bytes 26144 | tf_op jit(solution)/shard_map/while/body/eval_jaxpr/ppermute | solution.py:14
  24.4 0.6 copy-done.1
  25.0 0.2 multiply_reduce_fusion.6
  25.3 0.3 fusion.128
  26.1 0.6 slice-done
  26.6 0.3 fusion.131
  26.9 0.2 convolution_add_fusion.5
  27.2 1.3 %collective-permute-start.1 = (f32[16,408]{0,1:T(8,128)S(1)}, f32[16,408]{0,1:T(8,128)S(1)}, u32[]{:S(2)}, u32[]{:S(2)}) collective-permute-start(f32[16,408]{0,1:T(8,128)S(1)} %get-tuple-element.739), channel_id=1, source_target_pairs={{0,4},{4,8},{8,12},{12,0},{1,5},{5,9},{9,13},{13,1},{2,6},{6,10},{... | collective-permute-start | bytes 78344 | tf_op jit(solution)/shard_map/while/body/eval_jaxpr/ppermute | solution.py:14
  28.6 0.4 fusion.127
  29.1 3.5 %collective-permute-done = f32[16,2]{0,1:T(2,128)S(1)} collective-permute-done((f32[16,2]{0,1:T(2,128)S(1)}, f32[16,2]{0,1:T(2,128)S(1)}, u32[]{:S(2)}, u32[]{:S(2)}) %collective-permute-start) | collective-permute-done | bytes 160 | tf_op jit(solution)/shard_map/while/body/eval_jaxpr/ppermute | solution.py:14
  32.8 2.1 %collective-permute-done.1 = f32[16,408]{0,1:T(8,128)S(1)} collective-permute-done((f32[16,408]{0,1:T(8,128)S(1)}, f32[16,408]{0,1:T(8,128)S(1)}, u32[]{:S(2)}, u32[]{:S(2)}) %collective-permute-start.1) | collective-permute-done | bytes 26144 | tf_op jit(solution)/shard_map/while/body/eval_jaxpr/ppermute | solution.py:14
  35.0 0.6 copy-done.1
  35.6 0.2 multiply_reduce_fusion.6
  35.9 0.3 fusion.128
  36.6 0.6 slice-done
  37.2 0.3 fusion.131
  37.5 0.2 convolution_add_fusion.5
  37.8 0.6 collective-permute-start.1
  38.4 0.4 fusion.127
  38.9 4.2 %collective-permute-done = f32[16,2]{0,1:T(2,128)S(1)} collective-permute-done((f32[16,2]{0,1:T(2,128)S(1)}, f32[16,2]{0,1:T(2,128)S(1)}, u32[]{:S(2)}, u32[]{:S(2)}) %collective-permute-start) | collective-permute-done | bytes 160 | tf_op jit(solution)/shard_map/while/body/eval_jaxpr/ppermute | solution.py:14
  43.3 2.1 %collective-permute-done.1 = f32[16,408]{0,1:T(8,128)S(1)} collective-permute-done((f32[16,408]{0,1:T(8,128)S(1)}, f32[16,408]{0,1:T(8,128)S(1)}, u32[]{:S(2)}, u32[]{:S(2)}) %collective-permute-start.1) | collective-permute-done | bytes 26144 | tf_op jit(solution)/shard_map/while/body/eval_jaxpr/ppermute | solution.py:14
  45.6 0.6 copy-done.1
  46.2 0.2 multiply_reduce_fusion.6
  46.4 0.3 fusion.128
  47.2 0.6 slice-done
  47.8 0.3 fusion.131
  48.1 0.2 convolution_add_fusion.5
  48.4 1.8 %all-gather.5 = f32[2,32,6]{1,2,0:T(8,128)S(1)} all-gather(f32[1,32,6]{1,2,0:T(8,128)S(1)} %bitcast.274), channel_id=3, replica_groups=mesh['groups'=2,'blk'=4,'head'=2,'pair'=2] {'pair'}, dimensions={0}, use_global_device_ids=true | all-gather | bytes 2304 | tf_op jit(solution)/shard_map/all_gather | solution.py:18
  50.2 1.8 %all-gather.6 = f32[2,32,6]{1,2,0:T(8,128)S(1)} all-gather(f32[1,32,6]{1,2,0:T(8,128)S(1)} %bitcast.275), channel_id=4, replica_groups=mesh['groups'=2,'blk'=4,'head'=2,'pair'=2] {'pair'}, dimensions={0}, use_global_device_ids=true | all-gather | bytes 2304 | tf_op jit(solution)/shard_map/all_gather | solution.py:18
  52.3 1.9 %all-gather.4 = f32[64,6,128]{2,0,1:T(8,128)S(1)} all-gather(f32[32,6,128]{2,0,1:T(8,128)S(1)} %copy.216), channel_id=6, replica_groups=mesh['groups'=2,'blk'=4,'head'=2,'pair'=2] {'pair'}, dimensions={0}, use_global_device_ids=true | all-gather | bytes 294912 | tf_op jit(solution)/shard_map/all_gather | solution.py:18
  54.4 1.9 %all-gather = f32[64,6,16]{2,0,1:T(8,128)S(1)} all-gather(f32[32,6,16]{2,0,1:T(8,128)S(1)} %copy.206), channel_id=2, replica_groups=mesh['groups'=2,'blk'=4,'head'=2,'pair'=2] {'pair'}, dimensions={0}, use_global_device_ids=true | all-gather | bytes 36864 | tf_op jit(solution)/shard_map/all_gather | solution.py:18
  56.7 2.4 %all-gather.3 = f32[64,6,8,3]{2,1,3,0:T(8,128)S(1)} all-gather(f32[32,6,8,3]{2,1,3,0:T(8,128)S(1)} %copy.207), channel_id=5, replica_groups=mesh['groups'=2,'blk'=4,'head'=2,'pair'=2] {'pair'}, dimensions={0}, use_global_device_ids=true | all-gather | bytes 55296 | tf_op jit(solution)/shard_map/all_gather | solution.py:18
  59.1 0.3 fusion.30
  59.4 1.1 %fusion.82 = (bf16[32,6,8,3]{2,3,1,0:T(4,128)(2,1)S(1)}, f32[32,6,8]{2,1,0:T(8,128)S(1)}) fusion(f32[3,3,32,1]{0,1,3,2:T(4,128)S(1)} %copy.227, f32[32,6,8,3]{2,1,3,0:T(8,128)S(1)} %fusion.30), kind=kOutput, calls=%fused_computation.153 | convolution fusion | flops 178176 | bytes 34944 | tf_op jit(solution)/shard_map/abn,nhpa->nhpb/dot_general | solution.py:34
  61.0 0.4 convolution_bitcast_fusion.4
  61.4 8.6 %psum.7 = f32[32,384]{1,0:T(8,128)S(1)} all-reduce(f32[32,384]{1,0:T(8,128)S(1)} %convolution_bitcast_fusion.4), channel_id=1, replica_groups=mesh['groups'=2,'blk'=4,'head'=2,'pair'=2] {'head'}, use_global_device_ids=true, to_apply=%region_9.10 | all-reduce | flops 12288 | bytes 98304 | tf_op jit(solution)/shard_map/psum | solution.py:223
  70.5 0.6 copy-done.11
  71.3 0.4 copy-done.6
  71.9 0.3 convolution_bitcast_fusion.3
  72.4 5.4 %collective-permute-done.2 = f32[12,32]{1,0:T(8,128)S(1)} collective-permute-done((f32[12,32]{1,0:T(8,128)S(1)}, f32[12,32]{1,0:T(8,128)S(1)}, u32[]{:S(2)}, u32[]{:S(2)}) %collective-permute-start.2) | collective-permute-done | bytes 1568 | tf_op jit(solution)/shard_map/ppermute | solution.py:234
  77.9 5.4 %collective-permute-done.3 = f32[12,32]{1,0:T(8,128)S(1)} collective-permute-done((f32[12,32]{1,0:T(8,128)S(1)}, f32[12,32]{1,0:T(8,128)S(1)}, u32[]{:S(2)}, u32[]{:S(2)}) %collective-permute-start.3) | collective-permute-done | bytes 1568 | tf_op jit(solution)/shard_map/ppermute | solution.py:234
  83.3 5.4 %collective-permute-done.4 = f32[12,32]{1,0:T(8,128)S(1)} collective-permute-done((f32[12,32]{1,0:T(8,128)S(1)}, f32[12,32]{1,0:T(8,128)S(1)}, u32[]{:S(2)}, u32[]{:S(2)}) %collective-permute-start.4) | collective-permute-done | bytes 1568 | tf_op jit(solution)/shard_map/ppermute | solution.py:234
  88.8 0.7 constant_dynamic-slice_fusion.1
  (165 shorter events, 8.8 us)
Async XLA Ops:
  0.6 60.4 %copy-start = (bf16[6,176,384]{2,1,0:T(8,128)(2,1)S(1)}, bf16[6,176,384]{2,1,0:T(8,128)(2,1)}, u32[]{:S(2)}) copy-start(bf16[6,176,384]{2,1,0:T(8,128)(2,1)} %param.29) | copy-start | bytes 2433028
  0.7 0.7 copy-start.13
  0.7 1.6 %copy-start.9 = (f32[12,32]{1,0:T(8,128)S(1)}, f32[12,32]{1,0:T(8,128)}, u32[]{:S(2)}) copy-start(f32[12,32]{1,0:T(8,128)} %param.19) | copy-start | bytes 4612
  1.5 0.7 copy-start.14
  2.3 0.7 copy-start.3
  4.6 0.9 %copy-start.4 = (bf16[384,216]{0,1:T(8,128)(2,1)S(1)}, bf16[384,216]{0,1:T(8,128)(2,1)}, u32[]{:S(2)}) copy-start(bf16[384,216]{0,1:T(8,128)(2,1)} %param.25) | copy-start | bytes 497668
  6.1 1.0 %copy-start.5 = (bf16[384,192]{0,1:T(8,128)(2,1)S(1)}, bf16[384,192]{0,1:T(8,128)(2,1)}, u32[]{:S(2)}) copy-start(bf16[384,192]{0,1:T(8,128)(2,1)} %param.23) | copy-start | bytes 442372
  6.3 0.7 copy-start.15
  7.1 0.9 %copy-start.8 = (bf16[384,96]{0,1:T(8,128)(2,1)S(1)}, bf16[384,96]{0,1:T(8,128)(2,1)}, u32[]{:S(2)}) copy-start(bf16[384,96]{0,1:T(8,128)(2,1)} %param.22) | copy-start | bytes 221188
  8.1 1.1 %copy-start.2 = (bf16[32,4,16,128]{3,2,1,0:T(8,128)(2,1)S(1)}, bf16[32,4,16,128]{3,2,1,0:T(8,128)(2,1)}, u32[]{:S(2)}) copy-start(bf16[32,4,16,128]{3,2,1,0:T(8,128)(2,1)} %param.18) | copy-start | bytes 1572868
  8.8 0.7 copy-start.7
  10.7 0.7 copy-start.10
  12.8 6.7 %collective-permute-start = (f32[16,2]{0,1:T(2,128)S(1)}, f32[16,2]{0,1:T(2,128)S(1)}, u32[]{:S(2)}, u32[]{:S(2)}) collective-permute-start(f32[16,2]{0,1:T(2,128)S(1)} %get-tuple-element.740), channel_id=1, source_target_pairs={{0,4},{4,8},{8,12},{12,0},{1,5},{5,9},{9,13},{13,1},{2,6},{6,10},{... | collective-permute-start | bytes 392 | tf_op jit(solution)/shard_map/while/body/eval_jaxpr/ppermute | solution.py:14
  15.9 8.4 %collective-permute-start.1 = (f32[16,408]{0,1:T(8,128)S(1)}, f32[16,408]{0,1:T(8,128)S(1)}, u32[]{:S(2)}, u32[]{:S(2)}) collective-permute-start(f32[16,408]{0,1:T(8,128)S(1)} %get-tuple-element.739), channel_id=1, source_target_pairs={{0,4},{4,8},{8,12},{12,0},{1,5},{5,9},{9,13},{13,1},{2,6},{6,10},{... | collective-permute-start | bytes 78344 | tf_op jit(solution)/shard_map/while/body/eval_jaxpr/ppermute | solution.py:14
  24.4 0.7 copy-start.1
  25.7 0.9 slice-start
  27.2 5.4 %collective-permute-start = (f32[16,2]{0,1:T(2,128)S(1)}, f32[16,2]{0,1:T(2,128)S(1)}, u32[]{:S(2)}, u32[]{:S(2)}) collective-permute-start(f32[16,2]{0,1:T(2,128)S(1)} %get-tuple-element.740), channel_id=1, source_target_pairs={{0,4},{4,8},{8,12},{12,0},{1,5},{5,9},{9,13},{13,1},{2,6},{6,10},{... | collective-permute-start | bytes 392 | tf_op jit(solution)/shard_map/while/body/eval_jaxpr/ppermute | solution.py:14
  27.2 7.7 %collective-permute-start.1 = (f32[16,408]{0,1:T(8,128)S(1)}, f32[16,408]{0,1:T(8,128)S(1)}, u32[]{:S(2)}, u32[]{:S(2)}) collective-permute-start(f32[16,408]{0,1:T(8,128)S(1)} %get-tuple-element.739), channel_id=1, source_target_pairs={{0,4},{4,8},{8,12},{12,0},{1,5},{5,9},{9,13},{13,1},{2,6},{6,10},{... | collective-permute-start | bytes 78344 | tf_op jit(solution)/shard_map/while/body/eval_jaxpr/ppermute | solution.py:14
  35.0 0.7 copy-start.1
  36.3 0.9 slice-start
  37.8 5.4 %collective-permute-start = (f32[16,2]{0,1:T(2,128)S(1)}, f32[16,2]{0,1:T(2,128)S(1)}, u32[]{:S(2)}, u32[]{:S(2)}) collective-permute-start(f32[16,2]{0,1:T(2,128)S(1)} %get-tuple-element.740), channel_id=1, source_target_pairs={{0,4},{4,8},{8,12},{12,0},{1,5},{5,9},{9,13},{13,1},{2,6},{6,10},{... | collective-permute-start | bytes 392 | tf_op jit(solution)/shard_map/while/body/eval_jaxpr/ppermute | solution.py:14
  37.8 7.7 %collective-permute-start.1 = (f32[16,408]{0,1:T(8,128)S(1)}, f32[16,408]{0,1:T(8,128)S(1)}, u32[]{:S(2)}, u32[]{:S(2)}) collective-permute-start(f32[16,408]{0,1:T(8,128)S(1)} %get-tuple-element.739), channel_id=1, source_target_pairs={{0,4},{4,8},{8,12},{12,0},{1,5},{5,9},{9,13},{13,1},{2,6},{6,10},{... | collective-permute-start | bytes 78344 | tf_op jit(solution)/shard_map/while/body/eval_jaxpr/ppermute | solution.py:14
  45.5 0.7 copy-start.1
  46.9 0.9 slice-start
  61.0 9.3 %copy-start.12 = (f32[384]{0:T(512)S(1)}, f32[384]{0:T(512)}, u32[]{:S(2)}) copy-start(f32[384]{0:T(512)} %param.30) | copy-start | bytes 4612
  70.4 0.7 copy-start.11
  71.1 0.6 copy-start.6
  72.4 5.5 %collective-permute-start.2 = (f32[12,32]{1,0:T(8,128)S(1)}, f32[12,32]{1,0:T(8,128)S(1)}, u32[]{:S(2)}, u32[]{:S(2)}) collective-permute-start(f32[12,32]{1,0:T(8,128)S(1)} %pad_maximum_fusion.1), channel_id=1, source_target_pairs={{0,4},{4,8},{8,12},{12,0},{1,5},{5,9},{9,13},{13,1},{2,6},{6,10},{... | collective-permute-start | bytes 4616 | tf_op jit(solution)/shard_map/ppermute | solution.py:234
  77.9 5.4 %collective-permute-start.3 = (f32[12,32]{1,0:T(8,128)S(1)}, f32[12,32]{1,0:T(8,128)S(1)}, u32[]{:S(2)}, u32[]{:S(2)}) collective-permute-start(f32[12,32]{1,0:T(8,128)S(1)} %collective-permute-done.2), channel_id=1, source_target_pairs={{0,4},{4,8},{8,12},{12,0},{1,5},{5,9},{9,13},{13,1},{2,6},{6,10},{... | collective-permute-start | bytes 4616 | tf_op jit(solution)/shard_map/ppermute | solution.py:234
  83.3 5.4 %collective-permute-start.4 = (f32[12,32]{1,0:T(8,128)S(1)}, f32[12,32]{1,0:T(8,128)S(1)}, u32[]{:S(2)}, u32[]{:S(2)}) collective-permute-start(f32[12,32]{1,0:T(8,128)S(1)} %collective-permute-done.3), channel_id=1, source_target_pairs={{0,4},{4,8},{8,12},{12,0},{1,5},{5,9},{9,13},{13,1},{2,6},{6,10},{... | collective-permute-start | bytes 4616 | tf_op jit(solution)/shard_map/ppermute | solution.py:234
